TPU v7x, 128 devices: a whole 4x4x4 slice. The times are simulated.
128 devices in a mesh: gx: 8 (over x, core), gy: 16 (over y, z).
Axes of the slice: x: 4, y: 4, z: 4, core: 2. Of those that a mesh axis runs over, the one named last changes fastest.
Arguments:
- adjoint_state: float32 [4, 50, 128, 2048], P(None, None, 'gx', 'gy'), may hold values from -6 to 6
- velocity: float32 [2, 50, 128, 2048], P(None, None, 'gx', 'gy'), may hold values from -1.5 to 1.5
- diffusivity: float32 [128, 2048], P('gx', 'gy'), may hold values from 0.02 to 0.2
- mixing: float32 [128, 2048], P('gx', 'gy'), may hold values from 0.1 to 10
- wet_levels: int32 [128, 2048], P('gx', 'gy'), may hold values from 0 to 50
- innovations: float32 [262144, 128], P(('gx', 'gy')), may hold values from -6 to 6
- owner_tile: int32 [262144, 1], P(('gx', 'gy')), may hold values from 0 to 127; in each aligned block of 2048 rows (0 to 2047, 2048 to 4095, ...) at most 24 rows name the same one
- cell_index: int32 [262144], P(('gx', 'gy')), may hold values from 0 to 1904
- offsets: float32 [2, 262144], P(None, ('gx', 'gy')), may hold values from 0 to 1
- live_counts: int32 [128], P(('gx', 'gy')), may hold values from 1 to 2048, 196608 in all
- depth_weights: float32 [64, 50], replicated, may hold values from -0.75 to 0.75
Outputs:
- adjoint_result: float32 [4, 50, 128, 2048], P(None, None, 'gx', 'gy')
Inputs may be any that keep to these rules, and one draw needn't show every extreme that they name: owner_tile[o, 0] is the index gx * 16 + gy of the tile that holds observation o; among the 2048 rows of one device, in use or not, no tile is named more than 24 times. cell_index[o] = i * 127 + j names local cell (i, j) of the owning tile, so that all four corner cells lie in that tile. The first live_counts[s] rows of device s are in use.
All inputs are finite; a program needn't handle non-finite values.
Results may differ from a plain program's by a relative error of at most 0.0001.
Values sent between devices are 32-bit elements; how exact they have to be, the bound alone decides.
A program may use at most 128 MiB of HBM per device.

v0:
```python
import functools

import jax
import jax.numpy as jnp
from jax import lax
from jax.experimental import pallas as pl
from jax.experimental.pallas import tpu as pltpu
from jax.sharding import PartitionSpec as P

F32 = jnp.float32
BF16 = jnp.bfloat16
MESH = pl.DeviceIdType.MESH

PRESSURE_HEAT = 0.2
PRESSURE_SALT = 0.15
CORIOLIS_PEAK = 0.2

CAP = 24
LANES = 128
SUB = 8
PAD = 4


def split(value):
    high = value.astype(BF16)
    return high, (value - high.astype(F32)).astype(BF16)


def pack_kernel(
    live_ref, target_ref, cell_ref, offset_ref, rows_ref, weights_ref, send_ref, packed, slots, *, tiles, levels, deep
):
    obs = rows_ref.shape[0]
    prof = weights_ref.shape[0]
    block = send_ref.shape[0]
    step = pl.program_id(0)

    @pl.when(step == 0)
    def _():
        wide = jnp.concatenate([weights_ref[...], jnp.zeros((prof, LANES - levels), F32)], axis=1)
        both = jnp.concatenate([wide, pltpu.roll(wide, deep, 1)], axis=0)
        tri = (
            lax.broadcasted_iota(jnp.int32, (256, 256), 0) < lax.broadcasted_iota(jnp.int32, (256, 256), 1)
        ).astype(BF16)
        tile_place = lax.broadcasted_iota(jnp.int32, (tiles, 256), 0)
        carry = jnp.zeros((tiles, 1), F32)
        for part in range(obs // 256):
            span = slice(part * 256, (part + 1) * 256)
            place = lax.broadcasted_iota(jnp.int32, (1, 256), 1) + part * 256
            live = place < live_ref[0]
            target = target_ref[:, span]
            named = ((tile_place == target) & live).astype(F32)
            before = jnp.dot(named.astype(BF16), tri, preferred_element_type=F32) + carry
            rank = jnp.sum(named * before, axis=0, keepdims=True)
            carry = carry + jnp.sum(named, axis=1, keepdims=True)
            slots[:, span] = jnp.where(live, target * CAP + rank.astype(jnp.int32), -1)
            cell = cell_ref[:, span].astype(F32)
            row = jnp.floor((cell + 0.5) * (1.0 / 127.0))
            col = cell - 127.0 * row
            for half in range(2):
                cut = slice(half * LANES, (half + 1) * LANES)
                here = slice(part * 256 + half * LANES, part * 256 + (half + 1) * LANES)
                side = jnp.concatenate(
                    [
                        jnp.zeros((2 * deep, LANES), F32),
                        row[:, cut],
                        col[:, cut],
                        offset_ref[:, here],
                        jnp.zeros((LANES - 2 * deep - 4, LANES), F32),
                    ],
                    axis=0,
                )
                profile = jnp.dot(rows_ref[here, :], both, precision=lax.Precision.HIGHEST, preferred_element_type=F32)
                high, low = split(profile + side.T)
                packed[here, :LANES] = high
                packed[here, LANES:] = low

    slot_place = lax.broadcasted_iota(jnp.int32, (block, 1), 0) + step * block
    pick = (slot_place == slots[...]).astype(F32).astype(BF16)
    got = jnp.dot(pick, packed[...], preferred_element_type=F32)
    send_ref[...] = got[:, :LANES] + got[:, LANES:]


def pack(innovations, target, cell, offsets, live, weights, tiles, levels, deep):
    obs = innovations.shape[0]
    slots = tiles * CAP
    block = 256
    whole = lambda shape: pl.BlockSpec(shape, lambda i: (0,) * len(shape))
    return pl.pallas_call(
        functools.partial(pack_kernel, tiles=tiles, levels=levels, deep=deep),
        grid=(slots // block,),
        in_specs=[
            pl.BlockSpec(memory_space=pltpu.SMEM),
            whole((1, obs)),
            whole((1, obs)),
            whole((2, obs)),
            whole((obs, LANES)),
            whole(weights.shape),
        ],
        out_specs=pl.BlockSpec((block, LANES), lambda i: (i, 0)),
        out_shape=jax.ShapeDtypeStruct((slots, LANES), F32),
        scratch_shapes=[pltpu.VMEM((obs, 2 * LANES), BF16), pltpu.VMEM((1, obs), jnp.int32)],
        compiler_params=pltpu.CompilerParams(vmem_limit_bytes=48 << 20),
        name="pack_rows",
    )(live, target, cell, offsets, innovations, weights)


def scatter_kernel(rows_ref, forcing_ref, values, sides, columns, *, deep):
    count = rows_ref.shape[0]
    x = pl.program_id(0)

    @pl.when(x == 0)
    def _():
        lane = lax.broadcasted_iota(jnp.int32, (LANES, LANES), 1)
        y_place = lax.broadcasted_iota(jnp.int32, (LANES, LANES), 0).astype(F32)

        @pl.loop(0, count // LANES)
        def _(part):
            here = pl.ds(pl.multiple_of(part * LANES, LANES), LANES)
            block = rows_ref[here, :]
            high, low = split(jnp.where(lane < 2 * deep, block, 0.0))
            values[here, :LANES] = high
            values[here, LANES:] = low
            side = block.T[2 * deep : 2 * deep + SUB, :]
            sides[:, here] = side
            col, north = side[1:2, :], side[3:4, :]
            columns[:, here] = jnp.where(y_place == col, 1.0 - north, 0.0) + jnp.where(y_place == col + 1.0, north, 0.0)

    row, east = sides[0:1, :], sides[2:3, :]
    x_now = x.astype(F32)
    share = jnp.where(row == x_now, 1.0 - east, 0.0) + jnp.where(row + 1.0 == x_now, east, 0.0)
    high, low = split(columns[...] * share)
    got = jnp.dot(jnp.concatenate([high, low], axis=0), values[...], preferred_element_type=F32)
    plane = got[:LANES, :LANES] + got[:LANES, LANES:] + got[LANES:, :LANES]
    forcing_ref[0] = plane.T[: 2 * deep, :]


def scatter(rows, tile_rows, deep):
    count = rows.shape[0]
    return pl.pallas_call(
        functools.partial(scatter_kernel, deep=deep),
        grid=(tile_rows,),
        in_specs=[pl.BlockSpec((count, LANES), lambda i: (0, 0))],
        out_specs=pl.BlockSpec((1, 2 * deep, LANES), lambda i: (i, 0, 0)),
        out_shape=jax.ShapeDtypeStruct((tile_rows, 2 * deep, LANES), F32),
        scratch_shapes=[
            pltpu.VMEM((count, 2 * LANES), BF16),
            pltpu.VMEM((SUB, count), F32),
            pltpu.VMEM((LANES, count), F32),
        ],
        compiler_params=pltpu.CompilerParams(vmem_limit_bytes=48 << 20),
        name="scatter_rows",
    )(rows)


def steps_kernel(
    state_ref, forcing_ref, velocity_ref, diffusion_ref, mixing_ref, wet_ref, out_ref,
    field, east, north_a, north_b, north_m, north_p, kappa, result, inverse, gain, going,
    edge_lo, edge_hi, x_send, x_recv, y_send, y_recv, send_sem, recv_sem,
    *, levels, deep, span_x, span_y, total_rows,
):
    tile_x, tile_y = mixing_ref.shape
    rows = tile_x * deep
    wide = tile_x + 2 * PAD
    me_x, me_y = lax.axis_index("gx"), lax.axis_index("gy")
    west, right = lax.rem(me_x + span_x - 1, span_x), lax.rem(me_x + 1, span_x)
    south, up = lax.rem(me_y + span_y - 1, span_y), lax.rem(me_y + 1, span_y)
    peers = ((west, me_y), (right, me_y), (me_x, south), (me_x, up))

    barrier = pltpu.get_barrier_semaphore()
    for peer in peers:
        pl.semaphore_signal(barrier, inc=1, device_id=peer, device_id_type=MESH)

    mixing = mixing_ref[...]
    lane = lax.broadcasted_iota(jnp.int32, (1, tile_y), 1)
    third, twelfth = 8.0 / 12.0, 1.0 / 12.0

    def coefficient(l, q_before):
        diag = 1.0 + mixing * jnp.where((l == 0) | (l == levels - 1), 1.0, 2.0)
        q = 1.0 / (diag - mixing * mixing * q_before)
        inverse[l] = q
        gain[l] = mixing * q
        return q

    lax.fori_loop(0, levels, coefficient, jnp.zeros_like(mixing))

    zero_rows = jnp.zeros((PAD * deep, tile_y), F32)
    for c in range(4):
        field[c, : PAD * deep, :] = zero_rows
        field[c, (PAD + tile_x) * deep :, :] = zero_rows
    east[: PAD * deep, :] = zero_rows
    east[(PAD + tile_x) * deep :, :] = zero_rows
    kappa[...] = jnp.zeros_like(kappa)
    kappa[PAD : PAD + tile_x, :] = diffusion_ref[...]

    @pl.loop(0, deep - levels)
    def _(extra):
        blank = jnp.zeros((tile_x, tile_y), F32)
        for c in range(4):
            field[c, pl.ds(PAD * deep + levels + extra, tile_x, stride=deep), :] = blank
            result[c, pl.ds(levels + extra, tile_x, stride=deep), :] = blank
        east[pl.ds(PAD * deep + levels + extra, tile_x, stride=deep), :] = blank
        for table in (north_a, north_b, north_m, north_p):
            table[pl.ds(levels + extra, tile_x, stride=deep), :] = blank

    diffusion = diffusion_ref[...]
    mask_a = (lane >= 1).astype(F32)
    mask_b = (lane < tile_y - 1).astype(F32)
    mask_m = (lane >= 2).astype(F32)
    mask_p = (lane < tile_y - 2).astype(F32)

    @pl.loop(0, levels)
    def _(l):
        u, v = velocity_ref[0, l], velocity_ref[1, l]
        east[pl.ds(PAD * deep + l, tile_x, stride=deep), :] = u
        here = pl.ds(l, tile_x, stride=deep)
        north_a[here, :] = (third * v + diffusion) * mask_a
        north_b[here, :] = (diffusion - third * v) * mask_b
        north_m[here, :] = (twelfth * v) * mask_m
        north_p[here, :] = (twelfth * v) * mask_p

    @pl.loop(0, rows // LANES)
    def _(part):
        here = pl.ds(pl.multiple_of(part * LANES, LANES), LANES)
        edge_lo[0, :, here] = north_b[here, :].T[:SUB, :]
        edge_lo[1, :, here] = north_p[here, :].T[:SUB, :]
        edge_hi[0, :, here] = north_a[here, :].T[tile_y - SUB :, :]
        edge_hi[1, :, here] = north_m[here, :].T[tile_y - SUB :, :]

    cor = CORIOLIS_PEAK * (2.0 * ((lane + me_y * tile_y).astype(F32) + 0.5) / total_rows - 1.0)
    wet = wet_ref[...]
    pressure = (PRESSURE_HEAT, -PRESSURE_SALT)

    def x_part(c, x, t, push):
        def at(shift):
            return pl.ds(pl.multiple_of((x + shift) * deep, SUB) + t * SUB, SUB)

        def coef(shift):
            return third * east[at(shift), :], kappa[pl.ds(x + shift, 1), :]

        (flow_up, kap_up), (flow_down, kap_down) = coef(1), coef(-1)
        total = (
            (flow_up + kap_up) * field[c, at(1), :]
            + (kap_down - flow_down) * field[c, at(-1), :]
            - twelfth * (east[at(2), :] * field[c, at(2), :] - east[at(-2), :] * field[c, at(-2), :])
        )
        return total if push is None else total + pressure[c] * push

    def x_push(x, t):
        def at(shift):
            return pl.ds(pl.multiple_of((x + shift) * deep, SUB) + t * SUB, SUB)

        return third * (field[2, at(1), :] - field[2, at(-1), :]) - twelfth * (field[2, at(2), :] - field[2, at(-2), :])

    pl.semaphore_wait(barrier, 4)

    for turn in range(2):
        def down(l, before):
            now = []
            q, p = inverse[l], gain[l]
            under = l < wet
            for c in range(4):
                if turn == 0:
                    value = state_ref[c, l]
                    if c < 2:
                        value = value + forcing_ref[pl.ds(c * deep + l, tile_x, stride=2 * deep), :]
                else:
                    value = result[c, pl.ds(l, tile_x, stride=deep), :]
                value = jnp.where(under, value, 0.0) * q + p * before[c]
                going[c, l] = value
                now.append(value)
            return tuple(now)

        lax.fori_loop(0, levels, down, (jnp.zeros((tile_x, tile_y), F32),) * 4)

        def rise(k, below):
            l = levels - 1 - k
            p = jnp.where(k == 0, 0.0, 1.0) * gain[l]
            now = []
            for c in range(4):
                value = going[c, l] + p * below[c]
                field[c, pl.ds(PAD * deep + l, tile_x, stride=deep), :] = value
                now.append(value)
            return tuple(now)

        lax.fori_loop(0, levels, rise, (jnp.zeros((tile_x, tile_y), F32),) * 4)

        copies = []
        for side in range(2):
            for place in range(2):
                x = (PAD - 2 + place) if side == 0 else (PAD + tile_x + place)
                for t in range(deep // SUB):
                    push = x_push(x, t)
                    for c in range(4):
                        x_send[turn, side, place, c, t * SUB : (t + 1) * SUB, :] = x_part(c, x, t, push if c < 2 else None)
            copy = pltpu.make_async_remote_copy(
                src_ref=x_send.at[turn, side],
                dst_ref=x_recv.at[turn, side],
                send_sem=send_sem.at[turn, side],
                recv_sem=recv_sem.at[turn, side],
                device_id=peers[side],
                device_id_type=MESH,
            )
            copy.start()
            copies.append(copy)

        @pl.loop(0, rows // LANES)
        def _(part):
            here = pl.ds(pl.multiple_of(part * LANES, LANES), LANES)
            there = pl.ds(pl.multiple_of(part * LANES + PAD * deep, SUB), LANES)
            turned = [field[c, there, :].T for c in range(4)]
            b_lo, c_lo = edge_lo[0, :, here], edge_lo[1, :, here]
            a_hi, c_hi = edge_hi[0, :, here], edge_hi[1, :, here]
            a_lo, b_hi = b_lo + 16.0 * c_lo, a_hi - 16.0 * c_hi
            e_lo = [value[:SUB, :] for value in turned]
            e_hi = [value[tile_y - SUB :, :] for value in turned]
            for c in range(4):
                flow_a, flow_c = a_lo * e_lo[c], c_lo * e_lo[c]
                flow_b, flow_d = b_hi * e_hi[c], c_hi * e_hi[c]
                if c < 2:
                    flow_a = flow_a + pressure[c] * third * e_lo[3]
                    flow_c = flow_c + pressure[c] * twelfth * e_lo[3]
                    flow_b = flow_b - pressure[c] * third * e_hi[3]
                    flow_d = flow_d + pressure[c] * twelfth * e_hi[3]
                y_send[turn, 0, 2 * c : 2 * c + 1, here] = -flow_c[0:1, :]
                y_send[turn, 0, 2 * c + 1 : 2 * c + 2, here] = flow_a[0:1, :] - flow_c[1:2, :]
                y_send[turn, 1, 2 * c : 2 * c + 1, here] = flow_b[7:8, :] + flow_d[6:7, :]
                y_send[turn, 1, 2 * c + 1 : 2 * c + 2, here] = flow_d[7:8, :]

        for side in range(2):
            copy = pltpu.make_async_remote_copy(
                src_ref=y_send.at[turn, side],
                dst_ref=y_recv.at[turn, side],
                send_sem=send_sem.at[turn, 2 + side],
                recv_sem=recv_sem.at[turn, 2 + side],
                device_id=peers[2 + side],
                device_id_type=MESH,
            )
            copy.start()
            copies.append(copy)

        @pl.loop(0, tile_x)
        def _(row):
            x = row + PAD
            centre_weight = 1.0 - 4.0 * kappa[pl.ds(x, 1), :]
            for t in range(deep // SUB):
                at = pl.ds(pl.multiple_of(row * deep, SUB) + t * SUB, SUB)
                here = pl.ds(pl.multiple_of(x * deep, SUB) + t * SUB, SUB)
                e = [field[c, here, :] for c in range(4)]
                a, b, m, p = north_a[at, :], north_b[at, :], north_m[at, :], north_p[at, :]
                push = x_push(x, t)
                for c in range(4):
                    flow_a, flow_b, flow_m, flow_p = a * e[c], b * e[c], m * e[c], p * e[c]
                    if c < 2:
                        flow_a = flow_a + (pressure[c] * third * mask_a) * e[3]
                        flow_b = flow_b - (pressure[c] * third * mask_b) * e[3]
                        flow_m = flow_m + (pressure[c] * twelfth * mask_m) * e[3]
                        flow_p = flow_p + (pressure[c] * twelfth * mask_p) * e[3]
                    down_y = pltpu.roll(flow_a - pltpu.roll(flow_m, tile_y - 1, 1), tile_y - 1, 1)
                    up_y = pltpu.roll(flow_b + pltpu.roll(flow_p, 1, 1), 1, 1)
                    total = centre_weight * e[c] + x_part(c, x, t, push if c < 2 else None) + down_y + up_y
                    if c == 2:
                        total = total - cor * e[3]
                    if c == 3:
                        total = total + cor * e[2]
                    result[c, at, :] = total

        for copy in copies:
            copy.wait()

        from_east = (me_x < span_x - 1).astype(F32)
        from_west = (me_x > 0).astype(F32)
        for side, factor in ((0, from_east), (1, from_west)):
            for place in range(2):
                row = (tile_x - 2 + place) if side == 0 else place
                for c in range(4):
                    at = slice(row * deep, (row + 1) * deep)
                    result[c, at, :] = result[c, at, :] + factor * x_recv[turn, side, place, c]

        from_north = (me_y < span_y - 1).astype(F32)
        from_south = (me_y > 0).astype(F32)

        @pl.loop(0, rows // LANES)
        def _(part):
            here = pl.ds(pl.multiple_of(part * LANES, LANES), LANES)
            place = lax.broadcasted_iota(jnp.int32, (SUB, LANES), 0)
            got_north = y_recv[turn, 0, :, here] * from_north
            got_south = y_recv[turn, 1, :, here] * from_south
            for c in range(4):
                low = jnp.where(
                    place == 0, got_south[2 * c : 2 * c + 1, :], jnp.where(place == 1, got_south[2 * c + 1 : 2 * c + 2, :], 0.0)
                )
                high = jnp.where(
                    place == SUB - 2, got_north[2 * c : 2 * c + 1, :],
                    jnp.where(place == SUB - 1, got_north[2 * c + 1 : 2 * c + 2, :], 0.0),
                )
                whole = jnp.concatenate([low, jnp.zeros((tile_y - 2 * SUB, LANES), F32), high], axis=0)
                result[c, here, :] = result[c, here, :] + whole.T

    @pl.loop(0, levels)
    def _(l):
        under = l < wet
        for c in range(4):
            out_ref[c, l] = jnp.where(under, result[c, pl.ds(l, tile_x, stride=deep), :], 0.0)


def steps(state, forcing, velocity, diffusion, mixing, wet, deep, span_x, span_y):
    levels, tile_x, tile_y = state.shape[1:]
    rows = tile_x * deep
    wide = (tile_x + 2 * PAD) * deep
    vmem = pl.BlockSpec(memory_space=pltpu.VMEM)
    return pl.pallas_call(
        functools.partial(
            steps_kernel, levels=levels, deep=deep, span_x=span_x, span_y=span_y, total_rows=tile_y * span_y
        ),
        in_specs=[vmem] * 6,
        out_specs=vmem,
        out_shape=jax.ShapeDtypeStruct(state.shape, F32),
        scratch_shapes=[
            pltpu.VMEM((4, wide, tile_y), F32),
            pltpu.VMEM((wide, tile_y), F32),
            pltpu.VMEM((rows, tile_y), F32),
            pltpu.VMEM((rows, tile_y), F32),
            pltpu.VMEM((rows, tile_y), F32),
            pltpu.VMEM((rows, tile_y), F32),
            pltpu.VMEM((tile_x + 2 * PAD, tile_y), F32),
            pltpu.VMEM((4, rows, tile_y), F32),
            pltpu.VMEM((levels, tile_x, tile_y), F32),
            pltpu.VMEM((levels, tile_x, tile_y), F32),
            pltpu.VMEM((4, levels, tile_x, tile_y), F32),
            pltpu.VMEM((2, SUB, rows), F32),
            pltpu.VMEM((2, SUB, rows), F32),
            pltpu.VMEM((2, 2, 2, 4, deep, tile_y), F32),
            pltpu.VMEM((2, 2, 2, 4, deep, tile_y), F32),
            pltpu.VMEM((2, 2, SUB, rows), F32),
            pltpu.VMEM((2, 2, SUB, rows), F32),
            pltpu.SemaphoreType.DMA((2, 4)),
            pltpu.SemaphoreType.DMA((2, 4)),
        ],
        compiler_params=pltpu.CompilerParams(
            collective_id=0, has_side_effects=True, vmem_limit_bytes=56 << 20
        ),
        name="two_steps",
    )(state, forcing.reshape(-1, tile_y), velocity, diffusion, mixing, wet)


def on_device(
    adjoint_state, velocity, diffusivity, mixing, wet_levels, innovations, owner_tile, cell_index, offsets,
    live_counts, depth_weights,
):
    levels, tile_x, tile_y = adjoint_state.shape[1:]
    deep = -(-levels // SUB) * SUB
    span_x, span_y = lax.axis_size("gx"), lax.axis_size("gy")
    tiles = span_x * span_y
    sent = pack(
        innovations, owner_tile.reshape(1, -1), cell_index.reshape(1, -1), offsets, live_counts, depth_weights,
        tiles, levels, deep,
    )
    got = lax.all_to_all(sent.reshape(tiles, CAP, LANES), ("gx", "gy"), split_axis=0, concat_axis=0, tiled=True)
    forcing = scatter(got.reshape(tiles * CAP, LANES), tile_x, deep)
    return steps(adjoint_state, forcing, velocity, diffusivity, mixing, wet_levels, deep, span_x, span_y)


def solution(mesh):
    placed = (
        P(None, None, "gx", "gy"),
        P(None, None, "gx", "gy"),
        P("gx", "gy"),
        P("gx", "gy"),
        P("gx", "gy"),
        P(("gx", "gy"), None),
        P(("gx", "gy"), None),
        P(("gx", "gy")),
        P(None, ("gx", "gy")),
        P(("gx", "gy")),
        P(),
    )
    return jax.shard_map(
        on_device, mesh=mesh, in_specs=placed, out_specs=P(None, None, "gx", "gy"), check_vma=False
    )
```

profile of v0, /device:TPU:1, one launch (start us, length us, event | category | flops | bytes accessed | tf_op | source)
XLA Modules:
  0.0 87.2 jit_solution(6648138002206437866)
XLA Ops:
  0.7 0.8 copy.12.weights_ref
  1.5 0.0 copy-start.1
  1.5 1.2 %copy-done.1 = f32[2048,128]{1,0:T(8,128)S(1)} copy-done((f32[2048,128]{1,0:T(8,128)S(1)}, f32[2048,128]{1,0:T(8,128)}, u32[]{:S(2)}) %copy-start.1) | copy-done | bytes 1048600
  2.7 0.0 copy-start.2
  2.7 0.7 copy-done.2
  3.4 0.0 copy-start.3
  3.4 0.7 copy-done.3
  4.1 0.0 copy-start.4
  4.1 0.7 copy-done.4
  4.8 6.8 %pack_rows.1 = f32[3072,128]{1,0:T(8,128)S(1)} custom-call(s32[1]{0:T(128)S(6)} %copy.14.live_ref, s32[1,2048]{1,0:T(1,128)S(1)} %bitcast.8, s32[1,2048]{1,0:T(1,128)S(1)} %bitcast.9, f32[2,2048]{1,0:T(2,128)S(1)} %copy-done.2, f32[2048,128]{1,0:T(8,128)S(1)} %copy-done.1, f32[64,50]{1,0:T(8,128)S(1)} %copy.12.weights_ref), custom_call_target="tpu_custom_call" | custom-call | tf_op jit(solution)/shard_map/pack_rows/pallas_call | solution.py:88
  11.6 35.3 %all_to_all.5 = f32[128,24,128]{2,1,0:T(8,128)S(1)} all-to-all(f32[128,24,128]{2,1,0:T(8,128)S(1)} %bitcast.5), channel_id=1, replica_groups=mesh['gx'=8,'gy'=16] {'gx','gy'}, dimensions={0} | all-to-all | bytes 3145728 | tf_op jit(solution)/shard_map/all_to_all | solution.py:458
  46.9 13.2 %scatter_rows.1 = f32[16,112,128]{2,1,0:T(8,128)S(1)} custom-call(f32[3072,128]{1,0:T(8,128)S(1)} %bitcast.6), custom_call_target="tpu_custom_call" | custom-call | tf_op jit(solution)/shard_map/scatter_rows/pallas_call | solution.py:139
  60.1 0.0 copy-start
  60.1 0.9 %copy-done = f32[16,112,128]{2,1,0:T(8,128)} copy-done((f32[16,112,128]{2,1,0:T(8,128)}, f32[16,112,128]{2,1,0:T(8,128)S(1)}, u32[]{:S(2)}) %copy-start) | copy-done | bytes 917528
  61.0 23.4 %two_steps.1 = f32[4,50,16,128]{3,2,1,0:T(8,128)} custom-call(f32[4,50,16,128]{3,2,1,0:T(8,128)} %state_ref.1, f32[1792,128]{1,0:T(8,128)} %bitcast.7, f32[2,50,16,128]{3,2,1,0:T(8,128)} %velocity_ref.1, f32[16,128]{1,0:T(8,128)} %diffusion_ref.1, f32[16,128]{1,0:T(8,128)} %mixing_ref.1, s32[16,128]{1,0:T(8,128)} %wet_ref.1), custom_call_target="tpu_custom_call" | custom-call | tf_op jit(solution)/shard_map/two_steps/pallas_call | solution.py:411
  84.5 2.7 %copy.15 = f32[4,50,16,128]{3,2,1,0:T(8,128)} copy(f32[4,50,16,128]{3,2,1,0:T(8,128)} %two_steps.1) | data formatting | bytes 3276800
Async XLA Ops:
  1.5 1.2 %copy-start.1 = (f32[2048,128]{1,0:T(8,128)S(1)}, f32[2048,128]{1,0:T(8,128)}, u32[]{:S(2)}) copy-start(f32[2048,128]{1,0:T(8,128)} %rows_ref.1) | copy-start | bytes 3145732
  2.7 0.7 copy-start.2
  3.4 0.7 copy-start.3
  4.1 0.7 copy-start.4
  60.1 0.9 %copy-start = (f32[16,112,128]{2,1,0:T(8,128)}, f32[16,112,128]{2,1,0:T(8,128)S(1)}, u32[]{:S(2)}) copy-start(f32[16,112,128]{2,1,0:T(8,128)S(1)} %scatter_rows.1) | copy-start | bytes 2752516
where the time goes:
time: 87.6 us; the launch traced here: 87.2 us
  Pallas kernels  43.4 us (50%)
  blocking collectives  35.3 us (40%)
  local copies, waits for them, and re-layouts  7.82 us (9%)
    all_to_all x1, blocking collectives, on_device(): lax.all_to_all(sent.reshape(tiles, CAP, LANES), ('gx', 'gy'), split_axis=...  35.3 us
    pallas_call x1, Pallas kernels, steps(): pl.pallas_call(functools.partial(steps_kernel, levels=levels, deep=deep,...  23.4 us
    pallas_call x1, Pallas kernels, scatter(): pl.pallas_call(functools.partial(scatter_kernel, deep=deep), grid=(tile_r...  13.2 us
    unnamed x12, local copies, waits for them, and re-layouts  7.82 us
    pallas_call x1, Pallas kernels, pack(): pl.pallas_call(functools.partial(pack_kernel, tiles=tiles, levels=levels,...  6.78 us

commit v1 on v0

--- a/solution.py
+++ b/solution.py
@@ -26,150 +26,132 @@
     return high, (value - high.astype(F32)).astype(BF16)
 
 
-def pack_kernel(
-    live_ref, target_ref, cell_ref, offset_ref, rows_ref, weights_ref, send_ref, packed, slots, *, tiles, levels, deep
-):
-    obs = rows_ref.shape[0]
-    prof = weights_ref.shape[0]
-    block = send_ref.shape[0]
-    step = pl.program_id(0)
-
-    @pl.when(step == 0)
-    def _():
-        wide = jnp.concatenate([weights_ref[...], jnp.zeros((prof, LANES - levels), F32)], axis=1)
-        both = jnp.concatenate([wide, pltpu.roll(wide, deep, 1)], axis=0)
-        tri = (
-            lax.broadcasted_iota(jnp.int32, (256, 256), 0) < lax.broadcasted_iota(jnp.int32, (256, 256), 1)
-        ).astype(BF16)
-        tile_place = lax.broadcasted_iota(jnp.int32, (tiles, 256), 0)
-        carry = jnp.zeros((tiles, 1), F32)
-        for part in range(obs // 256):
-            span = slice(part * 256, (part + 1) * 256)
-            place = lax.broadcasted_iota(jnp.int32, (1, 256), 1) + part * 256
-            live = place < live_ref[0]
-            target = target_ref[:, span]
-            named = ((tile_place == target) & live).astype(F32)
-            before = jnp.dot(named.astype(BF16), tri, preferred_element_type=F32) + carry
-            rank = jnp.sum(named * before, axis=0, keepdims=True)
-            carry = carry + jnp.sum(named, axis=1, keepdims=True)
-            slots[:, span] = jnp.where(live, target * CAP + rank.astype(jnp.int32), -1)
-            cell = cell_ref[:, span].astype(F32)
-            row = jnp.floor((cell + 0.5) * (1.0 / 127.0))
-            col = cell - 127.0 * row
-            for half in range(2):
-                cut = slice(half * LANES, (half + 1) * LANES)
-                here = slice(part * 256 + half * LANES, part * 256 + (half + 1) * LANES)
-                side = jnp.concatenate(
-                    [
-                        jnp.zeros((2 * deep, LANES), F32),
-                        row[:, cut],
-                        col[:, cut],
-                        offset_ref[:, here],
-                        jnp.zeros((LANES - 2 * deep - 4, LANES), F32),
-                    ],
-                    axis=0,
-                )
-                profile = jnp.dot(rows_ref[here, :], both, precision=lax.Precision.HIGHEST, preferred_element_type=F32)
-                high, low = split(profile + side.T)
-                packed[here, :LANES] = high
-                packed[here, LANES:] = low
-
-    slot_place = lax.broadcasted_iota(jnp.int32, (block, 1), 0) + step * block
-    pick = (slot_place == slots[...]).astype(F32).astype(BF16)
-    got = jnp.dot(pick, packed[...], preferred_element_type=F32)
-    send_ref[...] = got[:, :LANES] + got[:, LANES:]
-
-
-def pack(innovations, target, cell, offsets, live, weights, tiles, levels, deep):
-    obs = innovations.shape[0]
-    slots = tiles * CAP
-    block = 256
-    whole = lambda shape: pl.BlockSpec(shape, lambda i: (0,) * len(shape))
-    return pl.pallas_call(
-        functools.partial(pack_kernel, tiles=tiles, levels=levels, deep=deep),
-        grid=(slots // block,),
-        in_specs=[
-            pl.BlockSpec(memory_space=pltpu.SMEM),
-            whole((1, obs)),
-            whole((1, obs)),
-            whole((2, obs)),
-            whole((obs, LANES)),
-            whole(weights.shape),
-        ],
-        out_specs=pl.BlockSpec((block, LANES), lambda i: (i, 0)),
-        out_shape=jax.ShapeDtypeStruct((slots, LANES), F32),
-        scratch_shapes=[pltpu.VMEM((obs, 2 * LANES), BF16), pltpu.VMEM((1, obs), jnp.int32)],
-        compiler_params=pltpu.CompilerParams(vmem_limit_bytes=48 << 20),
-        name="pack_rows",
-    )(live, target, cell, offsets, innovations, weights)
-
-
-def scatter_kernel(rows_ref, forcing_ref, values, sides, columns, *, deep):
-    count = rows_ref.shape[0]
-    x = pl.program_id(0)
-
-    @pl.when(x == 0)
-    def _():
-        lane = lax.broadcasted_iota(jnp.int32, (LANES, LANES), 1)
-        y_place = lax.broadcasted_iota(jnp.int32, (LANES, LANES), 0).astype(F32)
-
-        @pl.loop(0, count // LANES)
-        def _(part):
-            here = pl.ds(pl.multiple_of(part * LANES, LANES), LANES)
-            block = rows_ref[here, :]
-            high, low = split(jnp.where(lane < 2 * deep, block, 0.0))
-            values[here, :LANES] = high
-            values[here, LANES:] = low
-            side = block.T[2 * deep : 2 * deep + SUB, :]
-            sides[:, here] = side
-            col, north = side[1:2, :], side[3:4, :]
-            columns[:, here] = jnp.where(y_place == col, 1.0 - north, 0.0) + jnp.where(y_place == col + 1.0, north, 0.0)
-
-    row, east = sides[0:1, :], sides[2:3, :]
-    x_now = x.astype(F32)
-    share = jnp.where(row == x_now, 1.0 - east, 0.0) + jnp.where(row + 1.0 == x_now, east, 0.0)
-    high, low = split(columns[...] * share)
-    got = jnp.dot(jnp.concatenate([high, low], axis=0), values[...], preferred_element_type=F32)
-    plane = got[:LANES, :LANES] + got[:LANES, LANES:] + got[LANES:, :LANES]
-    forcing_ref[0] = plane.T[: 2 * deep, :]
-
-
-def scatter(rows, tile_rows, deep):
-    count = rows.shape[0]
-    return pl.pallas_call(
-        functools.partial(scatter_kernel, deep=deep),
-        grid=(tile_rows,),
-        in_specs=[pl.BlockSpec((count, LANES), lambda i: (0, 0))],
-        out_specs=pl.BlockSpec((1, 2 * deep, LANES), lambda i: (i, 0, 0)),
-        out_shape=jax.ShapeDtypeStruct((tile_rows, 2 * deep, LANES), F32),
-        scratch_shapes=[
-            pltpu.VMEM((count, 2 * LANES), BF16),
-            pltpu.VMEM((SUB, count), F32),
-            pltpu.VMEM((LANES, count), F32),
-        ],
-        compiler_params=pltpu.CompilerParams(vmem_limit_bytes=48 << 20),
-        name="scatter_rows",
-    )(rows)
-
-
-def steps_kernel(
-    state_ref, forcing_ref, velocity_ref, diffusion_ref, mixing_ref, wet_ref, out_ref,
+GROUP = 32
+BURST = 8
+
+
+def whole_kernel(
+    live_ref, target_hbm, cell_hbm, offset_hbm, rows_hbm, weights_hbm, state_hbm, velocity_hbm, diffusion_hbm,
+    mixing_hbm, wet_hbm, out_ref,
+    target_ref, cell_ref, offset_ref, rows_ref, weights_ref, state_ref, velocity_ref, diffusion_ref, mixing_ref,
+    wet_ref, packed, slots, send, recv, values, sides, columns, forcing_ref,
     field, east, north_a, north_b, north_m, north_p, kappa, result, inverse, gain, going,
-    edge_lo, edge_hi, x_send, x_recv, y_send, y_recv, send_sem, recv_sem,
+    edge_lo, edge_hi, x_send, x_recv, y_send, y_recv,
+    local_sem, row_send_sem, row_recv_sem, send_sem, recv_sem, ready_sem,
     *, levels, deep, span_x, span_y, total_rows,
 ):
     tile_x, tile_y = mixing_ref.shape
     rows = tile_x * deep
-    wide = tile_x + 2 * PAD
+    tiles = span_x * span_y
+    obs = rows_ref.shape[0]
+    prof = weights_ref.shape[1]
     me_x, me_y = lax.axis_index("gx"), lax.axis_index("gy")
     west, right = lax.rem(me_x + span_x - 1, span_x), lax.rem(me_x + 1, span_x)
     south, up = lax.rem(me_y + span_y - 1, span_y), lax.rem(me_y + 1, span_y)
     peers = ((west, me_y), (right, me_y), (me_x, south), (me_x, up))
 
+    moves = [
+        pltpu.make_async_copy(source, target, local_sem.at[place])
+        for place, (source, target) in enumerate(
+            (
+                (target_hbm, target_ref), (cell_hbm, cell_ref), (offset_hbm, offset_ref), (weights_hbm, weights_ref),
+                (rows_hbm, rows_ref), (mixing_hbm, mixing_ref), (diffusion_hbm, diffusion_ref), (wet_hbm, wet_ref),
+                (velocity_hbm, velocity_ref), (state_hbm, state_ref),
+            )
+        )
+    ]
+    for move in moves:
+        move.start()
+
     barrier = pltpu.get_barrier_semaphore()
-    for peer in peers:
+    row_peers = [(lax.rem(me_x + t, span_x), me_y) for t in range(1, span_x)]
+    column_peers = [(me_x, lax.rem(me_y + t, span_y)) for t in range(1, span_y)]
+    for peer in row_peers + column_peers:
         pl.semaphore_signal(barrier, inc=1, device_id=peer, device_id_type=MESH)
 
+    for move in moves[:5]:
+        move.wait()
+
+    wide = jnp.concatenate([weights_ref[...], jnp.zeros((levels, LANES - prof), F32)], axis=1)
+    gap = jnp.zeros((deep - levels, LANES), F32)
+    both = jnp.concatenate(
+        [wide, gap, pltpu.roll(wide, prof, 1), gap, jnp.zeros((LANES - 2 * deep, LANES), F32)], axis=0
+    ).T
+    tri = (
+        lax.broadcasted_iota(jnp.int32, (256, 256), 0) < lax.broadcasted_iota(jnp.int32, (256, 256), 1)
+    ).astype(BF16)
+    tile_place = lax.broadcasted_iota(jnp.int32, (tiles, 256), 0)
+    carry = jnp.zeros((tiles, 1), F32)
+    for part in range(obs // 256):
+        span = slice(part * 256, (part + 1) * 256)
+        place = lax.broadcasted_iota(jnp.int32, (1, 256), 1) + part * 256
+        live = place < live_ref[0]
+        target = target_ref[:, span]
+        named = ((tile_place == target) & live).astype(F32)
+        before = jnp.dot(named.astype(BF16), tri, preferred_element_type=F32) + carry
+        rank = jnp.sum(named * before, axis=0, keepdims=True)
+        carry = carry + jnp.sum(named, axis=1, keepdims=True)
+        slots[:, span] = jnp.where(live, target * CAP + rank.astype(jnp.int32), -1)
+        cell = cell_ref[:, span].astype(F32)
+        cell_row = jnp.floor((cell + 0.5) * (1.0 / (tile_y - 1)))
+        cell_col = cell - (tile_y - 1.0) * cell_row
+        for half in range(2):
+            cut = slice(half * LANES, (half + 1) * LANES)
+            here = slice(part * 256 + half * LANES, part * 256 + (half + 1) * LANES)
+            side = jnp.concatenate(
+                [
+                    jnp.zeros((2 * deep, LANES), F32), cell_row[:, cut], cell_col[:, cut], offset_ref[:, here],
+                    jnp.zeros((LANES - 2 * deep - 4, LANES), F32),
+                ],
+                axis=0,
+            )
+            profile = jnp.dot(rows_ref[here, :], both, precision=lax.Precision.HIGHEST, preferred_element_type=F32)
+            high, low = split(profile + side.T)
+            packed[here, :LANES] = high
+            packed[here, LANES:] = low
+
+    pl.semaphore_wait(barrier, len(row_peers) + len(column_peers))
+    for peer in column_peers:
+        pl.semaphore_signal(ready_sem, inc=1, device_id=peer, device_id_type=MESH)
+    pl.semaphore_wait(ready_sem, len(column_peers))
+
+    def peer_of(t):
+        dx = lax.rem(t, span_x)
+        return lax.rem(me_x + dx, span_x), lax.rem(me_y + t // span_x + 2 * dx, span_y)
+
+    def row_copy(t):
+        return pltpu.make_async_remote_copy(
+            src_ref=send.at[t], dst_ref=recv.at[t], send_sem=row_send_sem, recv_sem=row_recv_sem.at[t // GROUP],
+            device_id=peer_of(t), device_id_type=MESH,
+        )
+
+    @pl.loop(0, tiles // BURST)
+    def _(burst):
+        places = []
+        for r in range(BURST):
+            peer_x, peer_y = peer_of(burst * BURST + r)
+            base = (peer_x * span_y + peer_y) * CAP
+            places.append(lax.broadcasted_iota(jnp.int32, (CAP, 1), 0) + base)
+        pick = (jnp.concatenate(places, axis=0) == slots[...]).astype(F32).astype(BF16)
+        got = jnp.dot(pick, packed[...], preferred_element_type=F32)
+        got = got[:, :LANES] + got[:, LANES:]
+        for r in range(BURST):
+            send[burst * BURST + r] = got[r * CAP : (r + 1) * CAP]
+        for r in range(BURST):
+            if r == 0:
+
+                @pl.when(burst > 0)
+                def _():
+                    row_copy(burst * BURST).start()
+
+                @pl.when(burst == 0)
+                def _():
+                    recv[0] = got[:CAP]
+            else:
+                row_copy(burst * BURST + r).start()
+
+    for move in moves[5:9]:
+        move.wait()
     mixing = mixing_ref[...]
     lane = lax.broadcasted_iota(jnp.int32, (1, tile_y), 1)
     third, twelfth = 8.0 / 12.0, 1.0 / 12.0
@@ -251,7 +233,55 @@
 
         return third * (field[2, at(1), :] - field[2, at(-1), :]) - twelfth * (field[2, at(2), :] - field[2, at(-2), :])
 
-    pl.semaphore_wait(barrier, 4)
+
+    forcing_ref[...] = jnp.zeros_like(forcing_ref)
+    count = GROUP * CAP
+    y_place = lax.broadcasted_iota(jnp.int32, (tile_y, LANES), 0).astype(F32)
+    for group in range(tiles // GROUP):
+        first = 1 if group == 0 else 0
+        came = pl.ds(group * GROUP + first, GROUP - first)
+        pltpu.make_async_remote_copy(
+            src_ref=send.at[came], dst_ref=recv.at[came], send_sem=row_send_sem, recv_sem=row_recv_sem.at[group],
+            device_id=peers[0], device_id_type=MESH,
+        ).wait_recv()
+        table = recv[group * GROUP : (group + 1) * GROUP].reshape(count, LANES)
+        for part in range(count // LANES):
+            here = slice(part * LANES, (part + 1) * LANES)
+            turned = table[here].T
+            high, low = split(turned[: 2 * deep])
+            values[: 2 * deep, here] = high
+            values[2 * deep :, here] = low
+            side = turned[2 * deep : 2 * deep + SUB]
+            sides[:, here] = side
+            col, north = side[1:2, :], side[3:4, :]
+            columns[:, here] = jnp.where(y_place == col, 1.0 - north, 0.0) + jnp.where(y_place == col + 1.0, north, 0.0)
+
+        @pl.loop(0, tile_x // 2)
+        def _(pair):
+            cell_row, aside = sides[0:1, :], sides[2:3, :]
+            high, low = [], []
+            for half in range(2):
+                x_now = (2 * pair + half).astype(F32)
+                share = jnp.where(cell_row == x_now, 1.0 - aside, 0.0) + jnp.where(cell_row + 1.0 == x_now, aside, 0.0)
+                one, two = split(columns[...] * share)
+                high.append(one)
+                low.append(two)
+            across = (((1,), (1,)), ((), ()))
+            got = lax.dot_general(values[...], jnp.concatenate(high, axis=0), across, preferred_element_type=F32)
+            rest = lax.dot_general(
+                values[: 2 * deep], jnp.concatenate(low, axis=0), across, preferred_element_type=F32
+            )
+            total = got[: 2 * deep] + got[2 * deep :] + rest
+            for half in range(2):
+                at = pl.ds(pl.multiple_of((2 * pair + half) * (2 * deep), SUB), 2 * deep)
+                forcing_ref[at, :] = forcing_ref[at, :] + total[:, half * tile_y : (half + 1) * tile_y]
+
+    sent = pl.ds(1, tiles - 1)
+    pltpu.make_async_remote_copy(
+        src_ref=send.at[sent], dst_ref=recv.at[sent], send_sem=row_send_sem, recv_sem=row_recv_sem.at[0],
+        device_id=peers[0], device_id_type=MESH,
+    ).wait_send()
+    moves[9].wait()
 
     for turn in range(2):
         def down(l, before):
@@ -403,46 +433,6 @@
             out_ref[c, l] = jnp.where(under, result[c, pl.ds(l, tile_x, stride=deep), :], 0.0)
 
 
-def steps(state, forcing, velocity, diffusion, mixing, wet, deep, span_x, span_y):
-    levels, tile_x, tile_y = state.shape[1:]
-    rows = tile_x * deep
-    wide = (tile_x + 2 * PAD) * deep
-    vmem = pl.BlockSpec(memory_space=pltpu.VMEM)
-    return pl.pallas_call(
-        functools.partial(
-            steps_kernel, levels=levels, deep=deep, span_x=span_x, span_y=span_y, total_rows=tile_y * span_y
-        ),
-        in_specs=[vmem] * 6,
-        out_specs=vmem,
-        out_shape=jax.ShapeDtypeStruct(state.shape, F32),
-        scratch_shapes=[
-            pltpu.VMEM((4, wide, tile_y), F32),
-            pltpu.VMEM((wide, tile_y), F32),
-            pltpu.VMEM((rows, tile_y), F32),
-            pltpu.VMEM((rows, tile_y), F32),
-            pltpu.VMEM((rows, tile_y), F32),
-            pltpu.VMEM((rows, tile_y), F32),
-            pltpu.VMEM((tile_x + 2 * PAD, tile_y), F32),
-            pltpu.VMEM((4, rows, tile_y), F32),
-            pltpu.VMEM((levels, tile_x, tile_y), F32),
-            pltpu.VMEM((levels, tile_x, tile_y), F32),
-            pltpu.VMEM((4, levels, tile_x, tile_y), F32),
-            pltpu.VMEM((2, SUB, rows), F32),
-            pltpu.VMEM((2, SUB, rows), F32),
-            pltpu.VMEM((2, 2, 2, 4, deep, tile_y), F32),
-            pltpu.VMEM((2, 2, 2, 4, deep, tile_y), F32),
-            pltpu.VMEM((2, 2, SUB, rows), F32),
-            pltpu.VMEM((2, 2, SUB, rows), F32),
-            pltpu.SemaphoreType.DMA((2, 4)),
-            pltpu.SemaphoreType.DMA((2, 4)),
-        ],
-        compiler_params=pltpu.CompilerParams(
-            collective_id=0, has_side_effects=True, vmem_limit_bytes=56 << 20
-        ),
-        name="two_steps",
-    )(state, forcing.reshape(-1, tile_y), velocity, diffusion, mixing, wet)
-
-
 def on_device(
     adjoint_state, velocity, diffusivity, mixing, wet_levels, innovations, owner_tile, cell_index, offsets,
     live_counts, depth_weights,
@@ -451,13 +441,68 @@
     deep = -(-levels // SUB) * SUB
     span_x, span_y = lax.axis_size("gx"), lax.axis_size("gy")
     tiles = span_x * span_y
-    sent = pack(
-        innovations, owner_tile.reshape(1, -1), cell_index.reshape(1, -1), offsets, live_counts, depth_weights,
-        tiles, levels, deep,
+    obs = innovations.shape[0]
+    prof = depth_weights.shape[0]
+    rows = tile_x * deep
+    wide = (tile_x + 2 * PAD) * deep
+    hbm = pl.BlockSpec(memory_space=pltpu.HBM)
+    vmem = lambda *shape: pltpu.VMEM(shape, F32)
+    return pl.pallas_call(
+        functools.partial(
+            whole_kernel, levels=levels, deep=deep, span_x=span_x, span_y=span_y, total_rows=tile_y * span_y
+        ),
+        in_specs=[pl.BlockSpec(memory_space=pltpu.SMEM)] + [hbm] * 10,
+        out_specs=pl.BlockSpec(memory_space=pltpu.VMEM),
+        out_shape=jax.ShapeDtypeStruct(adjoint_state.shape, F32),
+        scratch_shapes=[
+            pltpu.VMEM((1, obs), jnp.int32),
+            pltpu.VMEM((1, obs), jnp.int32),
+            vmem(2, obs),
+            vmem(obs, LANES),
+            vmem(levels, prof),
+            vmem(4, levels, tile_x, tile_y),
+            vmem(2, levels, tile_x, tile_y),
+            vmem(tile_x, tile_y),
+            vmem(tile_x, tile_y),
+            pltpu.VMEM((tile_x, tile_y), jnp.int32),
+            pltpu.VMEM((obs, 2 * LANES), BF16),
+            pltpu.VMEM((1, obs), jnp.int32),
+            vmem(tiles, CAP, LANES),
+            vmem(tiles, CAP, LANES),
+            pltpu.VMEM((4 * deep, GROUP * CAP), BF16),
+            vmem(SUB, GROUP * CAP),
+            vmem(tile_y, GROUP * CAP),
+            vmem(tile_x * 2 * deep, tile_y),
+            vmem(4, wide, tile_y),
+            vmem(wide, tile_y),
+            vmem(rows, tile_y),
+            vmem(rows, tile_y),
+            vmem(rows, tile_y),
+            vmem(rows, tile_y),
+            vmem(tile_x + 2 * PAD, tile_y),
+            vmem(4, rows, tile_y),
+            vmem(levels, tile_x, tile_y),
+            vmem(levels, tile_x, tile_y),
+            vmem(4, levels, tile_x, tile_y),
+            vmem(2, SUB, rows),
+            vmem(2, SUB, rows),
+            vmem(2, 2, 2, 4, deep, tile_y),
+            vmem(2, 2, 2, 4, deep, tile_y),
+            vmem(2, 2, SUB, rows),
+            vmem(2, 2, SUB, rows),
+            pltpu.SemaphoreType.DMA((10,)),
+            pltpu.SemaphoreType.DMA,
+            pltpu.SemaphoreType.DMA((tiles // GROUP,)),
+            pltpu.SemaphoreType.DMA((2, 4)),
+            pltpu.SemaphoreType.DMA((2, 4)),
+            pltpu.SemaphoreType.REGULAR,
+        ],
+        compiler_params=pltpu.CompilerParams(collective_id=0, has_side_effects=True, vmem_limit_bytes=60 << 20),
+        name="whole",
+    )(
+        live_counts, owner_tile.reshape(1, obs), cell_index.reshape(1, obs), offsets, innovations, depth_weights.T,
+        adjoint_state, velocity, diffusivity, mixing, wet_levels,
     )
-    got = lax.all_to_all(sent.reshape(tiles, CAP, LANES), ("gx", "gy"), split_axis=0, concat_axis=0, tiled=True)
-    forcing = scatter(got.reshape(tiles * CAP, LANES), tile_x, deep)
-    return steps(adjoint_state, forcing, velocity, diffusivity, mixing, wet_levels, deep, span_x, span_y)
 
 
 def solution(mesh):

time: 87.6 us -> 59.7 us (0.68)
  blocking collectives: 35.3 us -> 0 us
  Pallas kernels: 43.4 us -> 56.2 us
  local copies, waits for them, and re-layouts: 7.82 us -> 2.74 us
    all_to_all x1 -> x0, blocking collectives: 35.3 us -> none  [on_device(): lax.all_to_all(sent.reshape(tiles, CAP, LANES), ('gx', 'gy'), split_axis=...]
    pallas_call x3 -> x1, Pallas kernels: 43.4 us -> 56.2 us  [on_device(): pl.pallas_call(functools.partial(whole_kernel, levels=levels, deep=deep,...]
    unnamed x12 -> x1, local copies, waits for them, and re-layouts: 7.82 us -> 2.74 us
where the time goes in v1:
time: 59.7 us; the launch traced here: 59.6 us
  Pallas kernels  56.2 us (94%)
  local copies, waits for them, and re-layouts  2.74 us (5%)
  between operations  0.66 us (1%)
    pallas_call x1, Pallas kernels, on_device(): pl.pallas_call(functools.partial(whole_kernel, levels=levels, deep=deep,...  56.2 us
    unnamed x1, local copies, waits for them, and re-layouts  2.74 us

profile of v1, /device:TPU:1, one launch (start us, length us, event | category | flops | bytes accessed | tf_op | source)
XLA Modules:
  0.0 59.6 jit_solution(5535578694120919863)
XLA Ops:
  0.7 56.2 %whole.1 = f32[4,50,16,128]{3,2,1,0:T(8,128)} custom-call(s32[1]{0:T(128)S(6)} %copy.13.live_ref, s32[1,2048]{1,0:T(1,128)} %bitcast.4, s32[1,2048]{1,0:T(1,128)} %bitcast.5, f32[2,2048]{1,0:T(2,128)} %offset_hbm.1, f32[2048,128]{1,0:T(8,128)} %rows_hbm.1, f32[50,64]{1,0:T(8,128)} %bitcast.3, f32[4,50,16,128]{3,2,1,0:T(8,128)} %state_hbm.1, ...), custom_call_target="tpu_custom_call" | custom-call | tf_op jit(solution)/shard_map/whole/pallas_call | solution.py:450
  56.8 2.7 %copy.14 = f32[4,50,16,128]{3,2,1,0:T(8,128)} copy(f32[4,50,16,128]{3,2,1,0:T(8,128)} %whole.1) | data formatting | bytes 3276800

commit v2 on v1

--- a/solution.py
+++ b/solution.py
@@ -28,6 +28,7 @@
 
 GROUP = 32
 BURST = 8
+AHEAD = 3
 
 
 def whole_kernel(
@@ -35,9 +36,9 @@
     mixing_hbm, wet_hbm, out_ref,
     target_ref, cell_ref, offset_ref, rows_ref, weights_ref, state_ref, velocity_ref, diffusion_ref, mixing_ref,
     wet_ref, packed, slots, send, recv, values, sides, columns, forcing_ref,
-    field, east, north_a, north_b, north_m, north_p, kappa, result, inverse, gain, going,
+    field, east_a, east_b, east_c, north_a, north_b, north_m, north_p, kappa, result, inverse, gain, going,
     edge_lo, edge_hi, x_send, x_recv, y_send, y_recv,
-    local_sem, row_send_sem, row_recv_sem, send_sem, recv_sem, ready_sem,
+    local_sem, row_send_sem, row_recv_sem, send_sem, recv_sem,
     *, levels, deep, span_x, span_y, total_rows,
 ):
     tile_x, tile_y = mixing_ref.shape
@@ -63,11 +64,13 @@
     for move in moves:
         move.start()
 
+    others = [
+        (lax.rem(me_x + t % span_x, span_x), lax.rem(me_y + t // span_x + 2 * (t % span_x), span_y))
+        for t in range(1, tiles)
+    ]
     barrier = pltpu.get_barrier_semaphore()
-    row_peers = [(lax.rem(me_x + t, span_x), me_y) for t in range(1, span_x)]
-    column_peers = [(me_x, lax.rem(me_y + t, span_y)) for t in range(1, span_y)]
-    for peer in row_peers + column_peers:
-        pl.semaphore_signal(barrier, inc=1, device_id=peer, device_id_type=MESH)
+    for other in others:
+        pl.semaphore_signal(barrier, inc=1, device_id=other, device_id_type=MESH)
 
     for move in moves[:5]:
         move.wait()
@@ -110,45 +113,29 @@
             packed[here, :LANES] = high
             packed[here, LANES:] = low
 
-    pl.semaphore_wait(barrier, len(row_peers) + len(column_peers))
-    for peer in column_peers:
-        pl.semaphore_signal(ready_sem, inc=1, device_id=peer, device_id_type=MESH)
-    pl.semaphore_wait(ready_sem, len(column_peers))
-
-    def peer_of(t):
-        dx = lax.rem(t, span_x)
-        return lax.rem(me_x + dx, span_x), lax.rem(me_y + t // span_x + 2 * dx, span_y)
-
-    def row_copy(t):
-        return pltpu.make_async_remote_copy(
-            src_ref=send.at[t], dst_ref=recv.at[t], send_sem=row_send_sem, recv_sem=row_recv_sem.at[t // GROUP],
-            device_id=peer_of(t), device_id_type=MESH,
-        )
-
-    @pl.loop(0, tiles // BURST)
-    def _(burst):
-        places = []
-        for r in range(BURST):
-            peer_x, peer_y = peer_of(burst * BURST + r)
-            base = (peer_x * span_y + peer_y) * CAP
-            places.append(lax.broadcasted_iota(jnp.int32, (CAP, 1), 0) + base)
-        pick = (jnp.concatenate(places, axis=0) == slots[...]).astype(F32).astype(BF16)
+    def send_burst(burst):
+        for t in range(burst * BURST, min((burst + 1) * BURST, len(others))):
+            pltpu.make_async_remote_copy(
+                src_ref=send.at[t], dst_ref=recv.at[t], send_sem=row_send_sem, recv_sem=row_recv_sem.at[t // GROUP],
+                device_id=others[t], device_id_type=MESH,
+            ).start()
+
+    named_tiles = others + [(me_x, me_y)]
+    for burst in range(tiles // BURST):
+        cut = slice(burst * BURST, (burst + 1) * BURST)
+        slot = lax.broadcasted_iota(jnp.int32, (CAP, 1), 0)
+        place = jnp.concatenate([slot + (x * span_y + y) * CAP for x, y in named_tiles[cut]], axis=0)
+        pick = (place == slots[...]).astype(F32).astype(BF16)
         got = jnp.dot(pick, packed[...], preferred_element_type=F32)
         got = got[:, :LANES] + got[:, LANES:]
-        for r in range(BURST):
-            send[burst * BURST + r] = got[r * CAP : (r + 1) * CAP]
-        for r in range(BURST):
-            if r == 0:
-
-                @pl.when(burst > 0)
-                def _():
-                    row_copy(burst * BURST).start()
-
-                @pl.when(burst == 0)
-                def _():
-                    recv[0] = got[:CAP]
-            else:
-                row_copy(burst * BURST + r).start()
+        send[cut] = got.reshape(BURST, CAP, LANES)
+        if burst == AHEAD - 1:
+            pl.semaphore_wait(barrier, len(others))
+            for early in range(AHEAD):
+                send_burst(early)
+        if burst >= AHEAD:
+            send_burst(burst)
+    recv[tiles - 1] = send[tiles - 1]
 
     for move in moves[5:9]:
         move.wait()
@@ -169,8 +156,9 @@
     for c in range(4):
         field[c, : PAD * deep, :] = zero_rows
         field[c, (PAD + tile_x) * deep :, :] = zero_rows
-    east[: PAD * deep, :] = zero_rows
-    east[(PAD + tile_x) * deep :, :] = zero_rows
+    for table in (east_a, east_b, east_c):
+        table[: PAD * deep, :] = zero_rows
+        table[(PAD + tile_x) * deep :, :] = zero_rows
     kappa[...] = jnp.zeros_like(kappa)
     kappa[PAD : PAD + tile_x, :] = diffusion_ref[...]
 
@@ -180,7 +168,8 @@
         for c in range(4):
             field[c, pl.ds(PAD * deep + levels + extra, tile_x, stride=deep), :] = blank
             result[c, pl.ds(levels + extra, tile_x, stride=deep), :] = blank
-        east[pl.ds(PAD * deep + levels + extra, tile_x, stride=deep), :] = blank
+        for table in (east_a, east_b, east_c):
+            table[pl.ds(PAD * deep + levels + extra, tile_x, stride=deep), :] = blank
         for table in (north_a, north_b, north_m, north_p):
             table[pl.ds(levels + extra, tile_x, stride=deep), :] = blank
 
@@ -193,7 +182,10 @@
     @pl.loop(0, levels)
     def _(l):
         u, v = velocity_ref[0, l], velocity_ref[1, l]
-        east[pl.ds(PAD * deep + l, tile_x, stride=deep), :] = u
+        there = pl.ds(PAD * deep + l, tile_x, stride=deep)
+        east_a[there, :] = third * u + diffusion
+        east_b[there, :] = diffusion - third * u
+        east_c[there, :] = twelfth * u
         here = pl.ds(l, tile_x, stride=deep)
         north_a[here, :] = (third * v + diffusion) * mask_a
         north_b[here, :] = (diffusion - third * v) * mask_b
@@ -209,37 +201,32 @@
         edge_hi[1, :, here] = north_m[here, :].T[tile_y - SUB :, :]
 
     cor = CORIOLIS_PEAK * (2.0 * ((lane + me_y * tile_y).astype(F32) + 0.5) / total_rows - 1.0)
+    full = (SUB, tile_y)
+    cor = jnp.broadcast_to(cor, full)
+    wide_a, wide_b = jnp.broadcast_to(third * mask_a, full), jnp.broadcast_to(third * mask_b, full)
+    wide_m, wide_p = jnp.broadcast_to(twelfth * mask_m, full), jnp.broadcast_to(twelfth * mask_p, full)
     wet = wet_ref[...]
     pressure = (PRESSURE_HEAT, -PRESSURE_SALT)
 
-    def x_part(c, x, t, push):
+    def x_parts(x, t):
         def at(shift):
             return pl.ds(pl.multiple_of((x + shift) * deep, SUB) + t * SUB, SUB)
 
-        def coef(shift):
-            return third * east[at(shift), :], kappa[pl.ds(x + shift, 1), :]
-
-        (flow_up, kap_up), (flow_down, kap_down) = coef(1), coef(-1)
-        total = (
-            (flow_up + kap_up) * field[c, at(1), :]
-            + (kap_down - flow_down) * field[c, at(-1), :]
-            - twelfth * (east[at(2), :] * field[c, at(2), :] - east[at(-2), :] * field[c, at(-2), :])
-        )
-        return total if push is None else total + pressure[c] * push
-
-    def x_push(x, t):
-        def at(shift):
-            return pl.ds(pl.multiple_of((x + shift) * deep, SUB) + t * SUB, SUB)
-
-        return third * (field[2, at(1), :] - field[2, at(-1), :]) - twelfth * (field[2, at(2), :] - field[2, at(-2), :])
-
+        up_1, down_1, up_2, down_2 = at(1), at(-1), at(2), at(-2)
+        a, b, c_up, c_down = east_a[up_1, :], east_b[down_1, :], east_c[up_2, :], east_c[down_2, :]
+        totals = []
+        for c in range(4):
+            e_up, e_down, e_up_2, e_down_2 = (field[c, place, :] for place in (up_1, down_1, up_2, down_2))
+            totals.append((a * e_up + b * e_down) + (c_down * e_down_2 - c_up * e_up_2))
+            if c == 2:
+                push = third * (e_up - e_down) - twelfth * (e_up_2 - e_down_2)
+        return [totals[0] + pressure[0] * push, totals[1] + pressure[1] * push, totals[2], totals[3]]
 
     forcing_ref[...] = jnp.zeros_like(forcing_ref)
     count = GROUP * CAP
     y_place = lax.broadcasted_iota(jnp.int32, (tile_y, LANES), 0).astype(F32)
     for group in range(tiles // GROUP):
-        first = 1 if group == 0 else 0
-        came = pl.ds(group * GROUP + first, GROUP - first)
+        came = pl.ds(group * GROUP, min(GROUP, len(others) - group * GROUP))
         pltpu.make_async_remote_copy(
             src_ref=send.at[came], dst_ref=recv.at[came], send_sem=row_send_sem, recv_sem=row_recv_sem.at[group],
             device_id=peers[0], device_id_type=MESH,
@@ -276,12 +263,20 @@
                 at = pl.ds(pl.multiple_of((2 * pair + half) * (2 * deep), SUB), 2 * deep)
                 forcing_ref[at, :] = forcing_ref[at, :] + total[:, half * tile_y : (half + 1) * tile_y]
 
-    sent = pl.ds(1, tiles - 1)
+    sent = pl.ds(0, len(others))
     pltpu.make_async_remote_copy(
         src_ref=send.at[sent], dst_ref=recv.at[sent], send_sem=row_send_sem, recv_sem=row_recv_sem.at[0],
         device_id=peers[0], device_id_type=MESH,
     ).wait_send()
     moves[9].wait()
+
+    def fives(body):
+        def run(k, carry):
+            for one in range(5):
+                carry = body(5 * k + one, carry)
+            return carry
+
+        return run
 
     for turn in range(2):
         def down(l, before):
@@ -300,7 +295,7 @@
                 now.append(value)
             return tuple(now)
 
-        lax.fori_loop(0, levels, down, (jnp.zeros((tile_x, tile_y), F32),) * 4)
+        lax.fori_loop(0, levels // 5, fives(down), (jnp.zeros((tile_x, tile_y), F32),) * 4)
 
         def rise(k, below):
             l = levels - 1 - k
@@ -312,16 +307,15 @@
                 now.append(value)
             return tuple(now)
 
-        lax.fori_loop(0, levels, rise, (jnp.zeros((tile_x, tile_y), F32),) * 4)
+        lax.fori_loop(0, levels // 5, fives(rise), (jnp.zeros((tile_x, tile_y), F32),) * 4)
 
         copies = []
         for side in range(2):
             for place in range(2):
                 x = (PAD - 2 + place) if side == 0 else (PAD + tile_x + place)
                 for t in range(deep // SUB):
-                    push = x_push(x, t)
-                    for c in range(4):
-                        x_send[turn, side, place, c, t * SUB : (t + 1) * SUB, :] = x_part(c, x, t, push if c < 2 else None)
+                    for c, part in enumerate(x_parts(x, t)):
+                        x_send[turn, side, place, c, t * SUB : (t + 1) * SUB, :] = part
             copy = pltpu.make_async_remote_copy(
                 src_ref=x_send.at[turn, side],
                 dst_ref=x_recv.at[turn, side],
@@ -371,40 +365,32 @@
         @pl.loop(0, tile_x)
         def _(row):
             x = row + PAD
-            centre_weight = 1.0 - 4.0 * kappa[pl.ds(x, 1), :]
+            centre_weight = jnp.broadcast_to(1.0 - 4.0 * kappa[pl.ds(x, 1), :], (SUB, tile_y))
             for t in range(deep // SUB):
                 at = pl.ds(pl.multiple_of(row * deep, SUB) + t * SUB, SUB)
                 here = pl.ds(pl.multiple_of(x * deep, SUB) + t * SUB, SUB)
                 e = [field[c, here, :] for c in range(4)]
                 a, b, m, p = north_a[at, :], north_b[at, :], north_m[at, :], north_p[at, :]
-                push = x_push(x, t)
+                push_a, push_b, push_m, push_p = wide_a * e[3], wide_b * e[3], wide_m * e[3], wide_p * e[3]
+                flow_x = x_parts(x, t)
                 for c in range(4):
                     flow_a, flow_b, flow_m, flow_p = a * e[c], b * e[c], m * e[c], p * e[c]
                     if c < 2:
-                        flow_a = flow_a + (pressure[c] * third * mask_a) * e[3]
-                        flow_b = flow_b - (pressure[c] * third * mask_b) * e[3]
-                        flow_m = flow_m + (pressure[c] * twelfth * mask_m) * e[3]
-                        flow_p = flow_p + (pressure[c] * twelfth * mask_p) * e[3]
-                    down_y = pltpu.roll(flow_a - pltpu.roll(flow_m, tile_y - 1, 1), tile_y - 1, 1)
-                    up_y = pltpu.roll(flow_b + pltpu.roll(flow_p, 1, 1), 1, 1)
-                    total = centre_weight * e[c] + x_part(c, x, t, push if c < 2 else None) + down_y + up_y
+                        flow_a = flow_a + pressure[c] * push_a
+                        flow_b = flow_b - pressure[c] * push_b
+                        flow_m = flow_m + pressure[c] * push_m
+                        flow_p = flow_p + pressure[c] * push_p
+                    down_y = pltpu.roll(flow_a, tile_y - 1, 1) - pltpu.roll(flow_m, tile_y - 2, 1)
+                    up_y = pltpu.roll(flow_b, 1, 1) + pltpu.roll(flow_p, 2, 1)
+                    total = (centre_weight * e[c] + flow_x[c]) + (down_y + up_y)
                     if c == 2:
                         total = total - cor * e[3]
                     if c == 3:
                         total = total + cor * e[2]
                     result[c, at, :] = total
 
-        for copy in copies:
+        for copy in copies[2:]:
             copy.wait()
-
-        from_east = (me_x < span_x - 1).astype(F32)
-        from_west = (me_x > 0).astype(F32)
-        for side, factor in ((0, from_east), (1, from_west)):
-            for place in range(2):
-                row = (tile_x - 2 + place) if side == 0 else place
-                for c in range(4):
-                    at = slice(row * deep, (row + 1) * deep)
-                    result[c, at, :] = result[c, at, :] + factor * x_recv[turn, side, place, c]
 
         from_north = (me_y < span_y - 1).astype(F32)
         from_south = (me_y > 0).astype(F32)
@@ -425,6 +411,18 @@
                 )
                 whole = jnp.concatenate([low, jnp.zeros((tile_y - 2 * SUB, LANES), F32), high], axis=0)
                 result[c, here, :] = result[c, here, :] + whole.T
+
+        for copy in copies[:2]:
+            copy.wait()
+
+        from_east = (me_x < span_x - 1).astype(F32)
+        from_west = (me_x > 0).astype(F32)
+        for side, factor in ((0, from_east), (1, from_west)):
+            for place in range(2):
+                row = (tile_x - 2 + place) if side == 0 else place
+                for c in range(4):
+                    at = slice(row * deep, (row + 1) * deep)
+                    result[c, at, :] = result[c, at, :] + factor * x_recv[turn, side, place, c]
 
     @pl.loop(0, levels)
     def _(l):
@@ -475,6 +473,8 @@
             vmem(tile_x * 2 * deep, tile_y),
             vmem(4, wide, tile_y),
             vmem(wide, tile_y),
+            vmem(wide, tile_y),
+            vmem(wide, tile_y),
             vmem(rows, tile_y),
             vmem(rows, tile_y),
             vmem(rows, tile_y),
@@ -495,7 +495,6 @@
             pltpu.SemaphoreType.DMA((tiles // GROUP,)),
             pltpu.SemaphoreType.DMA((2, 4)),
             pltpu.SemaphoreType.DMA((2, 4)),
-            pltpu.SemaphoreType.REGULAR,
         ],
         compiler_params=pltpu.CompilerParams(collective_id=0, has_side_effects=True, vmem_limit_bytes=60 << 20),
         name="whole",

time: 59.7 us -> 56.7 us (0.950)
  the two profiles are of different devices: /device:TPU:1 before, /device:TPU:8 now
where the time goes in v2:
time: 56.7 us; the launch traced here: 56.5 us
  Pallas kernels  53.1 us (94%)
  local copies, waits for them, and re-layouts  2.74 us (5%)
  between operations  0.66 us (1%)
    pallas_call x1, Pallas kernels, on_device(): pl.pallas_call(functools.partial(whole_kernel, levels=levels, deep=deep,...  53.1 us
    unnamed x1, local copies, waits for them, and re-layouts  2.74 us

profile of v2, /device:TPU:8, one launch (start us, length us, event | category | flops | bytes accessed | tf_op | source)
XLA Modules:
  0.0 56.5 jit_solution(6048405146754350550)
XLA Ops:
  0.7 53.1 %whole.1 = f32[4,50,16,128]{3,2,1,0:T(8,128)} custom-call(s32[1]{0:T(128)S(6)} %copy.13.live_ref, s32[1,2048]{1,0:T(1,128)} %bitcast.4, s32[1,2048]{1,0:T(1,128)} %bitcast.5, f32[2,2048]{1,0:T(2,128)} %offset_hbm.1, f32[2048,128]{1,0:T(8,128)} %rows_hbm.1, f32[50,64]{1,0:T(8,128)} %bitcast.3, f32[4,50,16,128]{3,2,1,0:T(8,128)} %state_hbm.1, ...), custom_call_target="tpu_custom_call" | custom-call | tf_op jit(solution)/shard_map/whole/pallas_call | solution.py:448
  53.8 2.7 %copy.14 = f32[4,50,16,128]{3,2,1,0:T(8,128)} copy(f32[4,50,16,128]{3,2,1,0:T(8,128)} %whole.1) | data formatting | bytes 3276800

commit v3 on v2

--- a/solution.py
+++ b/solution.py
@@ -28,14 +28,14 @@
 
 GROUP = 32
 BURST = 8
-AHEAD = 3
+AHEAD = 6
 
 
 def whole_kernel(
     live_ref, target_hbm, cell_hbm, offset_hbm, rows_hbm, weights_hbm, state_hbm, velocity_hbm, diffusion_hbm,
     mixing_hbm, wet_hbm, out_ref,
     target_ref, cell_ref, offset_ref, rows_ref, weights_ref, state_ref, velocity_ref, diffusion_ref, mixing_ref,
-    wet_ref, packed, slots, send, recv, values, sides, columns, forcing_ref,
+    wet_ref, packed, slots, send, recv, values, sides, columns,
     field, east_a, east_b, east_c, north_a, north_b, north_m, north_p, kappa, result, inverse, gain, going,
     edge_lo, edge_hi, x_send, x_recv, y_send, y_recv,
     local_sem, row_send_sem, row_recv_sem, send_sem, recv_sem,
@@ -137,7 +137,7 @@
             send_burst(burst)
     recv[tiles - 1] = send[tiles - 1]
 
-    for move in moves[5:9]:
+    for move in moves[5:]:
         move.wait()
     mixing = mixing_ref[...]
     lane = lax.broadcasted_iota(jnp.int32, (1, tile_y), 1)
@@ -181,6 +181,8 @@
 
     @pl.loop(0, levels)
     def _(l):
+        for c in range(4):
+            result[c, pl.ds(l, tile_x, stride=deep), :] = state_ref[c, l]
         u, v = velocity_ref[0, l], velocity_ref[1, l]
         there = pl.ds(PAD * deep + l, tile_x, stride=deep)
         east_a[there, :] = third * u + diffusion
@@ -222,7 +224,6 @@
                 push = third * (e_up - e_down) - twelfth * (e_up_2 - e_down_2)
         return [totals[0] + pressure[0] * push, totals[1] + pressure[1] * push, totals[2], totals[3]]
 
-    forcing_ref[...] = jnp.zeros_like(forcing_ref)
     count = GROUP * CAP
     y_place = lax.broadcasted_iota(jnp.int32, (tile_y, LANES), 0).astype(F32)
     for group in range(tiles // GROUP):
@@ -260,15 +261,16 @@
             )
             total = got[: 2 * deep] + got[2 * deep :] + rest
             for half in range(2):
-                at = pl.ds(pl.multiple_of((2 * pair + half) * (2 * deep), SUB), 2 * deep)
-                forcing_ref[at, :] = forcing_ref[at, :] + total[:, half * tile_y : (half + 1) * tile_y]
+                at = pl.ds(pl.multiple_of((2 * pair + half) * deep, SUB), deep)
+                for c in range(2):
+                    part = total[c * deep : (c + 1) * deep, half * tile_y : (half + 1) * tile_y]
+                    result[c, at, :] = result[c, at, :] + part
 
     sent = pl.ds(0, len(others))
     pltpu.make_async_remote_copy(
         src_ref=send.at[sent], dst_ref=recv.at[sent], send_sem=row_send_sem, recv_sem=row_recv_sem.at[0],
         device_id=peers[0], device_id_type=MESH,
     ).wait_send()
-    moves[9].wait()
 
     def fives(body):
         def run(k, carry):
@@ -278,18 +280,14 @@
 
         return run
 
-    for turn in range(2):
+    @pl.loop(0, 2)
+    def _(turn):
         def down(l, before):
             now = []
             q, p = inverse[l], gain[l]
             under = l < wet
             for c in range(4):
-                if turn == 0:
-                    value = state_ref[c, l]
-                    if c < 2:
-                        value = value + forcing_ref[pl.ds(c * deep + l, tile_x, stride=2 * deep), :]
-                else:
-                    value = result[c, pl.ds(l, tile_x, stride=deep), :]
+                value = result[c, pl.ds(l, tile_x, stride=deep), :]
                 value = jnp.where(under, value, 0.0) * q + p * before[c]
                 going[c, l] = value
                 now.append(value)
@@ -317,8 +315,8 @@
                     for c, part in enumerate(x_parts(x, t)):
                         x_send[turn, side, place, c, t * SUB : (t + 1) * SUB, :] = part
             copy = pltpu.make_async_remote_copy(
-                src_ref=x_send.at[turn, side],
-                dst_ref=x_recv.at[turn, side],
+                src_ref=x_send.at[turn, side, :, :, pl.ds(0, levels)],
+                dst_ref=x_recv.at[turn, side, :, :, pl.ds(0, levels)],
                 send_sem=send_sem.at[turn, side],
                 recv_sem=recv_sem.at[turn, side],
                 device_id=peers[side],
@@ -421,8 +419,8 @@
             for place in range(2):
                 row = (tile_x - 2 + place) if side == 0 else place
                 for c in range(4):
-                    at = slice(row * deep, (row + 1) * deep)
-                    result[c, at, :] = result[c, at, :] + factor * x_recv[turn, side, place, c]
+                    at = slice(row * deep, row * deep + levels)
+                    result[c, at, :] = result[c, at, :] + factor * x_recv[turn, side, place, c, :levels]
 
     @pl.loop(0, levels)
     def _(l):
@@ -470,7 +468,6 @@
             pltpu.VMEM((4 * deep, GROUP * CAP), BF16),
             vmem(SUB, GROUP * CAP),
             vmem(tile_y, GROUP * CAP),
-            vmem(tile_x * 2 * deep, tile_y),
             vmem(4, wide, tile_y),
             vmem(wide, tile_y),
             vmem(wide, tile_y),

time: 56.7 us -> 55.6 us (0.981)
  the two profiles are of different devices: /device:TPU:8 before, /device:TPU:1 now
where the time goes in v3:
time: 55.6 us; the launch traced here: 55.1 us
  Pallas kernels  51.7 us (93%)
  local copies, waits for them, and re-layouts  2.74 us (5%)
  between operations  0.66 us (1%)
    pallas_call x1, Pallas kernels, on_device(): pl.pallas_call(functools.partial(whole_kernel, levels=levels, deep=deep,...  51.7 us
    unnamed x1, local copies, waits for them, and re-layouts  2.74 us

profile of v3, /device:TPU:1, one launch (start us, length us, event | category | flops | bytes accessed | tf_op | source)
XLA Modules:
  0.0 55.1 jit_solution(3541230562252852947)
XLA Ops:
  0.7 51.7 %whole.1 = f32[4,50,16,128]{3,2,1,0:T(8,128)} custom-call(s32[1]{0:T(128)S(6)} %copy.13.live_ref, s32[1,2048]{1,0:T(1,128)} %bitcast.4, s32[1,2048]{1,0:T(1,128)} %bitcast.5, f32[2,2048]{1,0:T(2,128)} %offset_hbm.1, f32[2048,128]{1,0:T(8,128)} %rows_hbm.1, f32[50,64]{1,0:T(8,128)} %bitcast.3, f32[4,50,16,128]{3,2,1,0:T(8,128)} %state_hbm.1, ...), custom_call_target="tpu_custom_call" | custom-call | tf_op jit(solution)/shard_map/whole/pallas_call | solution.py:446
  52.4 2.7 %copy.14 = f32[4,50,16,128]{3,2,1,0:T(8,128)} copy(f32[4,50,16,128]{3,2,1,0:T(8,128)} %whole.1) | data formatting | bytes 3276800
